TPU v7x, 32 devices: a whole 2x2x4 slice. The times are simulated.
32 devices in a mesh: grp: 2 (over y), frm: 4 (over z), row: 4 (over x, core).
Axes of the slice: x: 2, y: 2, z: 4, core: 2. Of those that a mesh axis runs over, the one named last changes fastest.
Arguments:
- queries: bfloat16 [16, 8, 128, 2240], P(('grp', 'frm'), 'row'), parts along dimension 0, may hold values from -6 to 6
- keys: bfloat16 [16, 8, 128, 2240], P(('grp', 'frm'), 'row'), parts along dimension 0, may hold values from -6 to 6
- values: bfloat16 [16, 8, 128, 2240], P(('grp', 'frm'), 'row'), parts along dimension 0, may hold values from -6 to 6
- flags: int32 [16], P(('grp', 'frm')), parts along dimension 0, may hold values 0 or 1
- blocks: int32 [16], P(('grp', 'frm')), parts along dimension 0, may hold values from 0 to 2, as said below
- out_weight: bfloat16 [2240, 2240], P('frm'), may hold values from -0.125 to 0.125
- norm_gain: float32 [2240], replicated, may hold values from 0.1 to 1.9
Outputs:
- projected: bfloat16 [16, 8, 128, 2240], P(('grp', 'frm'), 'row'), parts along dimension 0
There are 2 independent parts, one for each index of `grp`. A program takes and returns all parts, laid end to end along the dimension named above; an argument that names none is the same for every part. Nothing has to cross between parts.
Inputs may be any that keep to these rules, and one draw needn't show every extreme that they name: `flags`: 1 marks a clean frame, 0 a noisy one. `blocks`: within the 8 frames of one group, block numbers never fall and each block is 1 to 4 consecutive frames, some block exactly 4; every number from 0 to 2 occurs.
All inputs are finite; a program needn't handle non-finite values. No bound on the sum of `flags` on one device may be relied on, other than what follows from the above.
Results may differ from a plain program's by a relative error of at most 0.0049.
Values may be sent and summed in bfloat16 or wider, within the bound.
No kernel may reach another device: no remote copies, remote signals or barrier semaphores. Data moves between devices by JAX's collectives and lax.ppermute only.
A program may use at most 192 MiB of HBM per device.

v0:
```python
import jax
import jax.numpy as jnp
from jax import lax
from jax.sharding import PartitionSpec as P

HEADS = 20
HD = 112
norm_eps = 1e-06


def entering(part, axis, combine, identity):
    place = lax.axis_index(axis)
    gathered = jax.tree.map(lambda a: lax.all_gather(a, axis), part)
    state = jax.tree.map(lambda a, e: jnp.zeros_like(a) + jnp.asarray(e, a.dtype), part, identity)

    def one(step, state):
        return combine(
            state, jax.tree.map(lambda a: lax.dynamic_index_in_dim(a, step, 0, False), gathered)
        )

    return lax.fori_loop(0, place, one, state)


def combine(earlier, later):
    closed_a, opened_a, latest_a = earlier
    closed_b, opened_b, latest_b = later
    advance = (latest_a < latest_b).astype(jnp.float32)
    return (
        closed_a + closed_b + advance * opened_a,
        opened_b + (1.0 - advance) * opened_a,
        jnp.maximum(latest_a, latest_b),
    )


def empty_carry(length):
    return (
        jnp.zeros((length,), jnp.float32),
        jnp.zeros((length,), jnp.float32),
        jnp.full((1,), -1.0, jnp.float32),
    )


def frame_element(frame_states, flag_values, block_values, frame_idx):
    length = frame_states.shape[1]
    return (
        jnp.zeros((length,), jnp.float32),
        flag_values[frame_idx] * frame_states[frame_idx],
        block_values[frame_idx : frame_idx + 1],
    )


def fold_frames(frame_states, flag_values, block_values):
    running = empty_carry(frame_states.shape[1])
    for frame_idx in range(frame_states.shape[0]):
        running = combine(
            running, frame_element(frame_states, flag_values, block_values, frame_idx)
        )
    return running


def read_frames(prefix, frame_states, flag_values, block_values):
    running = prefix
    collected = []
    for frame_idx in range(frame_states.shape[0]):
        advance = (running[2] < block_values[frame_idx : frame_idx + 1]).astype(jnp.float32)
        select = jnp.maximum(advance, flag_values[frame_idx])
        collected.append(running[0] + select * running[1] + frame_states[frame_idx])
        running = combine(
            running, frame_element(frame_states, flag_values, block_values, frame_idx)
        )
    return jnp.stack(collected)


def local(queries, keys, values, flags, blocks, out_weight, norm_gain):
    frames, lat_rows, lat_cols, model_width = queries.shape
    tokens = lat_rows * lat_cols
    key_pos = jax.nn.relu(keys).reshape(frames, tokens, HEADS, HD)
    value_heads = values.reshape(frames, tokens, HEADS, HD)
    partial_value = jnp.einsum(
        "ftha,fthb->fhab", key_pos, value_heads, preferred_element_type=jnp.float32
    )
    partial_value = partial_value.reshape(frames, HEADS * HD * HD)
    flag_values = flags.astype(jnp.float32)
    block_values = blocks.astype(jnp.float32)
    summed = lax.psum(partial_value, "row")
    totals = fold_frames(summed, flag_values, block_values)
    prefix = entering(
        (totals[0], totals[1], totals[2]), "frm", combine, empty_carry(summed.shape[1])
    )
    read_states = read_frames(prefix, summed, flag_values, block_values)
    read_tensor = read_states.reshape(frames, HEADS, HD, HD)
    query_pos = jax.nn.relu(queries).reshape(frames, tokens, HEADS, HD).astype(jnp.float32)
    attended = jnp.einsum(
        "ftha,fhab->fthb", query_pos, read_tensor, precision=lax.Precision.HIGHEST
    )
    inv_rms = lax.rsqrt(jnp.mean(attended * attended, axis=-1, keepdims=True) + norm_eps)
    gain_table = norm_gain.reshape(HEADS, HD)
    normed = (
        (attended * inv_rms * gain_table).astype(jnp.bfloat16).reshape(frames * tokens, model_width)
    )
    projected = jnp.dot(
        normed,
        lax.all_gather(out_weight, "frm", axis=0, tiled=True),
        preferred_element_type=jnp.float32,
    )
    return projected.astype(jnp.bfloat16).reshape(frames, lat_rows, lat_cols, model_width)


def solution(mesh):
    in_specs = (
        P(("grp", "frm"), "row", None, None),
        P(("grp", "frm"), "row", None, None),
        P(("grp", "frm"), "row", None, None),
        P(("grp", "frm")),
        P(("grp", "frm")),
        P("frm", None),
        P(),
    )
    out_specs = P(("grp", "frm"), "row", None, None)
    return jax.shard_map(local, mesh=mesh, in_specs=in_specs, out_specs=out_specs, check_vma=False)
```

profile of v0, /device:TPU:0, one launch (start us, length us, event | category | flops | bytes accessed | tf_op | source)
XLA Modules:
  0.0 476.6 jit_solution(3732474962754750551)
XLA Ops:
  8.3 10.3 %copy.16 = bf16[2,2,128,2240]{2,1,3,0:T(2,128)(2,1)} copy(bf16[2,2,128,2240]{2,3,1,0:T(8,128)(2,1)S(1)} %broadcast_maximum_fusion.1) | data formatting | bytes 4587520 | tf_op jit(solution)/shard_map/jit(relu)/max | solution.py:77
  18.7 5.2 %reshape.37 = bf16[2,256,20,112]{1,3,2,0:T(8,128)(2,1)S(1)} reshape(bf16[2,2,128,2240]{2,1,3,0:T(2,128)(2,1)} %copy.16) | data formatting | bytes 4587520 | tf_op jit(solution)/shard_map/reshape | solution.py:77
  23.9 12.6 %copy.17 = bf16[2,2,128,2240]{2,1,3,0:T(2,128)(2,1)} copy(bf16[2,2,128,2240]{2,3,1,0:T(8,128)(2,1)} %param.11) | data formatting | bytes 4587520 | tf_op args[2]
  36.5 6.2 %reshape.38 = bf16[2,256,20,112]{1,3,2,0:T(8,128)(2,1)} reshape(bf16[2,2,128,2240]{2,1,3,0:T(2,128)(2,1)} %copy.17) | data formatting | bytes 4587520 | tf_op jit(solution)/shard_map/reshape | solution.py:78
  42.7 3.8 fusion.10
  46.5 5.6 %reshape.39 = f32[2,250880]{1,0:T(2,128)} reshape(f32[2,20,112,112]{3,2,1,0:T(8,128)} %fusion.10) | data formatting | bytes 4014080 | tf_op jit(solution)/shard_map/reshape | solution.py:82
  56.6 48.6 %all-reduce.3.cloned.1.call-done = f32[2,250880]{1,0:T(2,128)} async-done(((f32[2,250880]{1,0:T(2,128)}), f32[2,250880]{1,0:T(2,128)}) %all-reduce.3.cloned.1.call-update) | async-done | bytes 2007056 | tf_op jit(solution)/shard_map/psum | solution.py:85
  105.1 8.0 %fusion.8 = (f32[1,250880]{1,0:T(1,128)S(1)}, f32[1,1,250880]{2,1,0:T(1,128)}, f32[1,1,250880]{2,1,0:T(1,128)}, f32[1,250880]{1,0:T(1,128)}) fusion(f32[2,250880]{1,0:T(2,128)} %all-reduce.3.cloned.1.call-done, f32[]{:T(128)} %bitcast.7, f32[]{:T(128)} %bitcast.6, f32[]{:T(128)} %bitcast.5, f32[]{:T(128)} %bitcast.12, f32[]{:T(128)} %bitcast.11), kind=kLoop, calls=%fused_computation.27 | loop fusion | flops 1505280 | bytes 6021140 | tf_op jit(solution)/shard_map/slice | solution.py:47
  114.4 11.9 %all-reduce = f32[4]{0:T(128)S(1)} all-reduce(f32[4]{0:T(128)S(1)} %get-tuple-element.81), channel_id=2, replica_groups=mesh['grp'=2,'frm'=4,'row'=4] {'frm'}, use_global_device_ids=true, to_apply=%add | all-reduce | flops 4 | bytes 32
  126.4 10.1 %copy.20 = bf16[2,2,128,2240]{2,1,3,0:T(2,128)(2,1)S(1)} copy(bf16[2,2,128,2240]{2,3,1,0:T(8,128)(2,1)S(1)} %broadcast_maximum_fusion) | data formatting | bytes 4587520 | tf_op jit(solution)/shard_map/jit(relu)/max | solution.py:92
  136.5 2.7 reshape.40
  139.3 51.7 %all-gather.11.cloned.1.call-done = f32[4,1,250880]{2,1,0:T(1,128)} async-done(((f32[1,1,250880]{2,1,0:T(1,128)}), f32[4,1,250880]{2,1,0:T(1,128)}) %all-gather.11.cloned.1.call-update) | async-done | bytes 4014096 | tf_op jit(solution)/shard_map/all_gather | solution.py:13
  191.1 5.5 %copy.28 = f32[4,1,250880]{2,0,1:T(4,128)} copy(f32[4,1,250880]{2,1,0:T(1,128)} %all-gather.11.cloned.1.call-done) | data formatting | bytes 8028160
  196.5 72.4 %all-gather.9.cloned.1.call-done = f32[4,1,250880]{2,1,0:T(1,128)} async-done(((f32[1,1,250880]{2,1,0:T(1,128)}), f32[4,1,250880]{2,1,0:T(1,128)}) %all-gather.9.cloned.1.call-update) | async-done | bytes 4014096 | tf_op jit(solution)/shard_map/all_gather | solution.py:13
  268.9 5.5 %copy.29 = f32[4,1,250880]{2,0,1:T(4,128)} copy(f32[4,1,250880]{2,1,0:T(1,128)} %all-gather.9.cloned.1.call-done) | data formatting | bytes 8028160
  277.9 3.6 add_add_fusion.1
  281.5 1.9 stack.9
  283.8 3.0 stack.10
  286.7 2.7 copy.19
  289.4 3.7 fusion
  293.9 2.4 copy.21
  296.7 153.4 %all-gather.7.cloned.1.call-done = bf16[2240,2240]{1,0:T(8,128)(2,1)} async-done(((bf16[560,2240]{1,0:T(8,128)(2,1)}), bf16[2240,2240]{1,0:T(8,128)(2,1)}) %all-gather.7.cloned.1.call-update) | async-done | bytes 10035216 | tf_op jit(solution)/shard_map/all_gather | solution.py:103
  450.1 13.4 %convolution_convert_fusion = bf16[512,2240]{0,1:T(8,128)(2,1)} fusion(bf16[512,2240]{0,1:T(8,128)(2,1)S(1)} %bitcast.74, bf16[2240,2240]{1,0:T(8,128)(2,1)} %all-gather.7.cloned.1.call-done), kind=kOutput, calls=%fused_computation.10 | convolution fusion | flops 5139169280 | bytes 14622720 | tf_op jit(solution)/shard_map/dot_general | solution.py:101
  463.6 4.8 %reshape.42 = bf16[2,2,128,2240]{2,1,0,3:T(2,128)(2,1)S(1)} reshape(bf16[512,2240]{0,1:T(8,128)(2,1)} %convolution_convert_fusion) | data formatting | bytes 4587520 | tf_op jit(solution)/shard_map/reshape | solution.py:106
  (37 shorter events, 9.5 us)
Async XLA Ops:
  6.5 98.6 %all-reduce.3.cloned.1.call-start = ((), (), s32[]{:S(2)}) async-start(), calls=%async_computation | async-start | bytes 4014080 | tf_op jit(solution)/shard_map/psum | solution.py:85
  46.5 5.6 %copy-start.3 = (s32[2]{0:T(128)S(1)}, s32[2]{0:T(128)}, u32[]{:S(2)}) copy-start(s32[2]{0:T(128)} %param.13) | copy-start | bytes 28
  46.5 5.7 %copy-start.5 = (u32[32]{0:T(128)S(1)}, u32[32]{0:T(128)}, u32[]{:S(2)}) copy-start(u32[32]{0:T(128)} %constant.52) | copy-start | bytes 388
  46.5 9.4 %copy-start.4 = (s32[2]{0:T(128)S(1)}, s32[2]{0:T(128)}, u32[]{:S(2)}) copy-start(s32[2]{0:T(128)} %param.12) | copy-start | bytes 28
  52.0 139.0 %all-gather.11.cloned.1.call-start = ((), (), s32[]{:S(2)}) async-start(), calls=%async_computation.3 | async-start | bytes 5017600 | tf_op jit(solution)/shard_map/all_gather | solution.py:13
  113.1 13.2 %copy-start.1 = (bf16[2,2,128,2240]{2,3,1,0:T(8,128)(2,1)S(1)}, bf16[2,2,128,2240]{2,3,1,0:T(8,128)(2,1)}, u32[]{:S(2)}) copy-start(bf16[2,2,128,2240]{2,3,1,0:T(8,128)(2,1)} %param.9) | copy-start | bytes 6881284
  113.1 155.8 %all-gather.9.cloned.1.call-start = ((), (), s32[]{:S(2)}) async-start(), calls=%async_computation.2 | async-start | bytes 5017600 | tf_op jit(solution)/shard_map/all_gather | solution.py:13
  113.8 336.3 %all-gather.7.cloned.1.call-start = ((), (), s32[]{:S(2)}) async-start(), calls=%async_computation.1 | async-start | bytes 12902400 | tf_op jit(solution)/shard_map/all_gather | solution.py:103
  136.5 2.8 copy-start.2
  283.8 5.7 %copy-start = (bf16[2,256,20,112]{1,3,2,0:T(8,128)(2,1)S(1)}, bf16[2,256,20,112]{1,3,2,0:T(8,128)(2,1)}, u32[]{:S(2)}) copy-start(bf16[2,256,20,112]{1,3,2,0:T(8,128)(2,1)} %reshape.40) | copy-start | bytes 6881284
Sparse Core Ops, SparseCore 0:
  52.2 52.9 all-reduce.2
  113.2 77.8 all-gather.10
  192.6 76.2 all-gather.8
  270.3 179.7 all-gather.6
where the time goes:
time: 477 us
  waiting for transfers between devices  327 us (69%)
  local copies, waits for them, and re-layouts  82.4 us (17%)
  matrix products  21 us (4%)
  between operations  18.3 us (4%)
  other arithmetic  15.5 us (3%)
  blocking collectives  11.9 us (2%)
    all_gather x1, waiting for transfers between devices, local(): lax.all_gather(out_weight, 'frm', axis=0, tiled=True)  153 us
    all_gather x2, waiting for transfers between devices, entering(): gathered = jax.tree.map(lambda a: lax.all_gather(a, axis), part)  124 us
    psum x1, waiting for transfers between devices, local(): summed = lax.psum(partial_value, 'row')  48.6 us
    unnamed x18, local copies, waits for them, and re-layouts  24.6 us
    dot_general x1, matrix products, local(): jnp.dot(normed, lax.all_gather(out_weight, 'frm', axis=0, tiled=True), pr...  13.4 us
    unnamed x1, blocking collectives  11.9 us
    max x1, local copies, waits for them, and re-layouts, local(): key_pos = jax.nn.relu(keys).reshape(frames, tokens, HEADS, HD)  10.3 us
    max x1, local copies, waits for them, and re-layouts, local(): jax.nn.relu(queries).reshape(frames, tokens, HEADS, HD).astype(jnp.float32)  10.1 us
  transfers between devices with their start and end apart: 4, of which 4 were waited for; matrix products, arithmetic and copies ran while one was open for 10% of the time, Pallas kernels for 0%

commit v1 on v0

--- a/solution.py
+++ b/solution.py
@@ -82,7 +82,7 @@
     partial_value = partial_value.reshape(frames, HEADS * HD * HD)
     flag_values = flags.astype(jnp.float32)
     block_values = blocks.astype(jnp.float32)
-    summed = lax.psum(partial_value, "row")
+    summed = jnp.sum(lax.all_gather(partial_value, "row"), axis=0)
     totals = fold_frames(summed, flag_values, block_values)
     prefix = entering(
         (totals[0], totals[1], totals[2]), "frm", combine, empty_carry(summed.shape[1])

time: 477 us -> 490 us (1.027)
  waiting for transfers between devices: 327 us -> 333 us
  other arithmetic: 15.5 us -> 21.3 us
    all_gather x0 -> x1, waiting for transfers between devices: none -> 54.6 us  [local(): summed = jnp.sum(lax.all_gather(partial_value, 'row'), axis=0)]
    psum x1 -> x0, waiting for transfers between devices: 48.6 us -> none  [local(): summed = lax.psum(partial_value, 'row')]
    reduce_sum x0 -> x1, other arithmetic: none -> 7.94 us  [local(): summed = jnp.sum(lax.all_gather(partial_value, 'row'), axis=0)]
    another operation x2 -> x3, local copies, waits for them, and re-layouts: 0.13 us -> 5.78 us  [the longest x1 5.64 us: local(): summed = jnp.sum(lax.all_gather(partial_value, 'row'), axis=0)]
    reshape x1 -> x0, local copies, waits for them, and re-layouts: 5.55 us -> none  [local(): partial_value = partial_value.reshape(frames, HEADS * HD * HD)]
  transfers between devices with their start and end apart: 4 -> 4, of which waited for: 4 -> 4; matrix products, arithmetic and copies ran while one was open for 10% -> 9% of each run, Pallas kernels for 0% -> 0%
where the time goes in v1:
time: 490 us; the launch traced here: 489 us
  waiting for transfers between devices  333 us (68%)
  local copies, waits for them, and re-layouts  82.5 us (17%)
  other arithmetic  21.3 us (4%)
  matrix products  21 us (4%)
  between operations  18.3 us (4%)
  blocking collectives  11.9 us (2%)
    all_gather x1, waiting for transfers between devices, local(): lax.all_gather(out_weight, 'frm', axis=0, tiled=True)  153 us
    all_gather x2, waiting for transfers between devices, entering(): gathered = jax.tree.map(lambda a: lax.all_gather(a, axis), part)  124 us
    all_gather x1, waiting for transfers between devices, local(): summed = jnp.sum(lax.all_gather(partial_value, 'row'), axis=0)  54.6 us
    unnamed x18, local copies, waits for them, and re-layouts  24.6 us
    dot_general x1, matrix products, local(): jnp.dot(normed, lax.all_gather(out_weight, 'frm', axis=0, tiled=True), pr...  13.4 us
    unnamed x1, blocking collectives  11.9 us
    max x1, local copies, waits for them, and re-layouts, local(): key_pos = jax.nn.relu(keys).reshape(frames, tokens, HEADS, HD)  10.3 us
    max x1, local copies, waits for them, and re-layouts, local(): jax.nn.relu(queries).reshape(frames, tokens, HEADS, HD).astype(jnp.float32)  10.1 us
  transfers between devices with their start and end apart: 4, of which 4 were waited for; matrix products, arithmetic and copies ran while one was open for 9% of the time, Pallas kernels for 0%

profile of v1, /device:TPU:0, one launch (start us, length us, event | category | flops | bytes accessed | tf_op | source)
XLA Modules:
  0.0 488.6 jit_solution(7940514945706562120)
XLA Ops:
  8.3 10.3 %copy.16 = bf16[2,2,128,2240]{2,1,3,0:T(2,128)(2,1)} copy(bf16[2,2,128,2240]{2,3,1,0:T(8,128)(2,1)S(1)} %broadcast_maximum_fusion.1) | data formatting | bytes 4587520 | tf_op jit(solution)/shard_map/jit(relu)/max | solution.py:77
  18.7 5.2 %reshape.34 = bf16[2,256,20,112]{1,3,2,0:T(8,128)(2,1)S(1)} reshape(bf16[2,2,128,2240]{2,1,3,0:T(2,128)(2,1)} %copy.16) | data formatting | bytes 4587520 | tf_op jit(solution)/shard_map/reshape | solution.py:77
  23.9 12.6 %copy.17 = bf16[2,2,128,2240]{2,1,3,0:T(2,128)(2,1)} copy(bf16[2,2,128,2240]{2,3,1,0:T(8,128)(2,1)} %param.11) | data formatting | bytes 4587520 | tf_op args[2]
  36.5 6.2 %reshape.35 = bf16[2,256,20,112]{1,3,2,0:T(8,128)(2,1)} reshape(bf16[2,2,128,2240]{2,1,3,0:T(2,128)(2,1)} %copy.17) | data formatting | bytes 4587520 | tf_op jit(solution)/shard_map/reshape | solution.py:78
  42.7 3.8 fusion.10
  46.5 5.6 %all_gather_reshape.3 = f32[1,2,250880]{2,1,0:T(2,128)} reshape(f32[2,20,112,112]{3,2,1,0:T(8,128)} %fusion.10) | data formatting | bytes 4014080 | tf_op jit(solution)/shard_map/all_gather;reshape | solution.py:85
  56.6 54.6 %all-gather.8.cloned.1.call-done = f32[4,2,250880]{2,1,0:T(2,128)} async-done(((f32[1,2,250880]{2,1,0:T(2,128)}), f32[4,2,250880]{2,1,0:T(2,128)}) %all-gather.8.cloned.1.call-update) | async-done | bytes 8028176 | tf_op jit(solution)/shard_map/all_gather | solution.py:85
  111.2 7.9 %reduce_sum.18 = f32[2,250880]{1,0:T(2,128)S(1)} reduce(f32[4,2,250880]{2,1,0:T(2,128)} %all-gather.8.cloned.1.call-done, f32[]{:T(128)} %constant.35.clone.1), dimensions={0}, to_apply=%region_0.1 | reduce | flops 1505280 | bytes 10035204 | tf_op jit(solution)/shard_map/reduce_sum | solution.py:85
  119.2 5.9 %fusion.8 = (f32[1,250880]{1,0:T(1,128)S(1)}, f32[1,1,250880]{2,1,0:T(1,128)}, f32[1,1,250880]{2,1,0:T(1,128)}, f32[1,250880]{1,0:T(1,128)}) fusion(f32[2,250880]{1,0:T(2,128)S(1)} %reduce_sum.18, f32[]{:T(128)} %bitcast.7, f32[]{:T(128)} %bitcast.6, f32[]{:T(128)} %bitcast.5, f32[]{:T(128)} %bitcast.12, f32[]{:T(128)} %bitcast.11), kind=kLoop, calls=%fused_computation.27 | loop fusion | flops 1505280 | bytes 6021140 | tf_op jit(solution)/shard_map/slice | solution.py:47
  126.4 11.9 %all-reduce = f32[4]{0:T(128)S(1)} all-reduce(f32[4]{0:T(128)S(1)} %get-tuple-element.81), channel_id=2, replica_groups=mesh['grp'=2,'frm'=4,'row'=4] {'frm'}, use_global_device_ids=true, to_apply=%add | all-reduce | flops 4 | bytes 32
  138.4 10.1 %copy.20 = bf16[2,2,128,2240]{2,1,3,0:T(2,128)(2,1)S(1)} copy(bf16[2,2,128,2240]{2,3,1,0:T(8,128)(2,1)S(1)} %broadcast_maximum_fusion) | data formatting | bytes 4587520 | tf_op jit(solution)/shard_map/jit(relu)/max | solution.py:92
  148.5 2.7 reshape.36
  151.3 51.7 %all-gather.14.cloned.1.call-done = f32[4,1,250880]{2,1,0:T(1,128)} async-done(((f32[1,1,250880]{2,1,0:T(1,128)}), f32[4,1,250880]{2,1,0:T(1,128)}) %all-gather.14.cloned.1.call-update) | async-done | bytes 4014096 | tf_op jit(solution)/shard_map/all_gather | solution.py:13
  203.0 5.5 %copy.28 = f32[4,1,250880]{2,0,1:T(4,128)} copy(f32[4,1,250880]{2,1,0:T(1,128)} %all-gather.14.cloned.1.call-done) | data formatting | bytes 8028160
  208.5 72.4 %all-gather.12.cloned.1.call-done = f32[4,1,250880]{2,1,0:T(1,128)} async-done(((f32[1,1,250880]{2,1,0:T(1,128)}), f32[4,1,250880]{2,1,0:T(1,128)}) %all-gather.12.cloned.1.call-update) | async-done | bytes 4014096 | tf_op jit(solution)/shard_map/all_gather | solution.py:13
  280.9 5.5 %copy.29 = f32[4,1,250880]{2,0,1:T(4,128)} copy(f32[4,1,250880]{2,1,0:T(1,128)} %all-gather.12.cloned.1.call-done) | data formatting | bytes 8028160
  289.9 3.6 add_add_fusion.1
  295.7 3.0 stack.10
  298.7 2.7 copy.19
  301.4 3.7 fusion
  305.8 2.4 copy.21
  308.7 153.4 %all-gather.10.cloned.1.call-done = bf16[2240,2240]{1,0:T(8,128)(2,1)} async-done(((bf16[560,2240]{1,0:T(8,128)(2,1)}), bf16[2240,2240]{1,0:T(8,128)(2,1)}) %all-gather.10.cloned.1.call-update) | async-done | bytes 10035216 | tf_op jit(solution)/shard_map/all_gather | solution.py:103
  462.1 13.4 %convolution_convert_fusion = bf16[512,2240]{0,1:T(8,128)(2,1)} fusion(bf16[512,2240]{0,1:T(8,128)(2,1)S(1)} %bitcast.74, bf16[2240,2240]{1,0:T(8,128)(2,1)} %all-gather.10.cloned.1.call-done), kind=kOutput, calls=%fused_computation.10 | convolution fusion | flops 5139169280 | bytes 14622720 | tf_op jit(solution)/shard_map/dot_general | solution.py:101
  475.5 4.8 reshape.38
  (38 shorter events, 11.4 us)
Async XLA Ops:
  6.5 104.7 %all-gather.8.cloned.1.call-start = ((), (), s32[]{:S(2)}) async-start(), calls=%async_computation | async-start | bytes 10035200 | tf_op jit(solution)/shard_map/all_gather | solution.py:85
  46.5 5.7 %copy-start.3 = (s32[2]{0:T(128)S(1)}, s32[2]{0:T(128)}, u32[]{:S(2)}) copy-start(s32[2]{0:T(128)} %param.13) | copy-start | bytes 28
  46.5 5.8 %copy-start.5 = (u32[32]{0:T(128)S(1)}, u32[32]{0:T(128)}, u32[]{:S(2)}) copy-start(u32[32]{0:T(128)} %constant.52) | copy-start | bytes 388
  46.5 9.5 %copy-start.4 = (s32[2]{0:T(128)S(1)}, s32[2]{0:T(128)}, u32[]{:S(2)}) copy-start(s32[2]{0:T(128)} %param.12) | copy-start | bytes 28
  52.1 150.9 %all-gather.14.cloned.1.call-start = ((), (), s32[]{:S(2)}) async-start(), calls=%async_computation.3 | async-start | bytes 5017600 | tf_op jit(solution)/shard_map/all_gather | solution.py:13
  125.0 13.2 %copy-start.1 = (bf16[2,2,128,2240]{2,3,1,0:T(8,128)(2,1)S(1)}, bf16[2,2,128,2240]{2,3,1,0:T(8,128)(2,1)}, u32[]{:S(2)}) copy-start(bf16[2,2,128,2240]{2,3,1,0:T(8,128)(2,1)} %param.9) | copy-start | bytes 6881284
  125.1 155.8 %all-gather.12.cloned.1.call-start = ((), (), s32[]{:S(2)}) async-start(), calls=%async_computation.2 | async-start | bytes 5017600 | tf_op jit(solution)/shard_map/all_gather | solution.py:13
  125.8 336.3 %all-gather.10.cloned.1.call-start = ((), (), s32[]{:S(2)}) async-start(), calls=%async_computation.1 | async-start | bytes 12902400 | tf_op jit(solution)/shard_map/all_gather | solution.py:103
  148.5 2.8 copy-start.2
  295.7 5.7 %copy-start = (bf16[2,256,20,112]{1,3,2,0:T(8,128)(2,1)S(1)}, bf16[2,256,20,112]{1,3,2,0:T(8,128)(2,1)}, u32[]{:S(2)}) copy-start(bf16[2,256,20,112]{1,3,2,0:T(8,128)(2,1)} %reshape.36) | copy-start | bytes 6881284
Sparse Core Ops, SparseCore 0:
  52.3 58.9 all-gather.7
  125.2 77.8 all-gather.13
  204.6 76.2 all-gather.11
  282.3 179.7 all-gather.9
